TPU v7x, 256 devices: a whole 4x4x8 slice. The times are simulated.
256 devices in a mesh: dp: 2 (over x_lo), expert: 8 (over z), shard: 16 (over x_hi, y, core).
Axes of the slice: x: 4 (x_hi: 2, x_lo: 2; x = x_hi * 2 + x_lo), y: 4, z: 8, core: 2. Of those that a mesh axis runs over, the one named last changes fastest.
Arguments:
- tokens: bfloat16 [2048, 6144], P(('dp', 'expert', 'shard')), may hold values from -6 to 6
- gate_up_weight: bfloat16 [8, 2, 8192, 6144], P(None, None, ('dp', 'expert', 'shard')), may hold values from -0.078125 to 0.078125
- down_weight: bfloat16 [8, 8192, 6144], P(None, ('dp', 'expert', 'shard')), may hold values from -0.0625 to 0.0625
- expert_ids: int32 [2048, 2], P(('dp', 'expert', 'shard')), may hold values from 0 to 7, as said below
- slot_ids: int32 [2048, 2], P(('dp', 'expert', 'shard')), may hold values from 0 to 3, as said below
- gate_values: float32 [2048, 2], P(('dp', 'expert', 'shard')), may hold values from 0.1 to 1
- old_place: int32 [8], replicated, may hold values from 0 to 7, each once
- new_place: int32 [8], replicated, may hold values from 0 to 7, each once
Outputs:
- mixed_out: bfloat16 [2048, 6144], P(('dp', 'expert', 'shard'))
Inputs may be any that keep to these rules, and one draw needn't show every extreme that they name: `expert_ids`: each token names 2 different experts; among the 8 tokens of one block no expert is named more than 4 times, and one expert is named exactly 4 times in every block. `slot_ids`: within one block, two choices that name the same expert have different slots. `old_place`: each expert number appears once. `new_place`: each expert number appears once.
All inputs are finite; a program needn't handle non-finite values.
Results may differ from a plain program's by a relative error of at most 0.02.
Values may be sent and summed in bfloat16 or wider, within the bound.
A program may use at most 128 MiB of HBM per device.

v0:
```python
import jax
import jax.numpy as jnp
from jax import lax
from jax.sharding import PartitionSpec as P


def placement_order(old_place, new_place):
    slot_total = old_place.shape[0]
    matches = (new_place[:, None] == old_place[None, :]).astype(jnp.int32)
    return jnp.sum(matches * jnp.arange(slot_total, dtype=jnp.int32)[None, :], axis=1)


def swiglu_rows(row_block, pair_weight):
    gate_up = jnp.einsum("rd,gud->rgu", row_block, pair_weight, preferred_element_type=jnp.float32)
    return (jax.nn.silu(gate_up[:, 0]) * gate_up[:, 1]).astype(jnp.bfloat16)


def local(
    tokens, gate_up_weight, down_weight, expert_ids, slot_ids, gate_values, old_place, new_place
):
    experts = gate_up_weight.shape[0]
    sliver = gate_up_weight.shape[2]
    model_width = tokens.shape[1]
    tok_rows = tokens.shape[0]
    choices_per_token = expert_ids.shape[1]
    capacity = 2 * tok_rows * choices_per_token // experts
    cell_count = experts * capacity
    data_ways = lax.axis_size("dp")
    slot_order = placement_order(old_place, new_place)
    cell_ids = expert_ids * capacity + slot_ids
    cell_range = jnp.arange(cell_count, dtype=jnp.int32)
    cell_hits = (cell_ids[:, :, None] == cell_range[None, None, :]).astype(jnp.float32)
    token_picks = jnp.sum(cell_hits, axis=1)
    dispatched = jnp.dot(
        token_picks.T.astype(jnp.bfloat16), tokens, preferred_element_type=jnp.float32
    ).astype(jnp.bfloat16)
    received = lax.all_to_all(
        dispatched.reshape(experts, capacity, model_width),
        "expert",
        split_axis=0,
        concat_axis=0,
        tiled=True,
    )
    own_rows = received.reshape(cell_count, model_width)
    sectioned_in = gate_up_weight.reshape(experts, 2, data_ways, sliver // data_ways, model_width)
    sectioned_down = down_weight.reshape(experts, 1, data_ways, sliver // data_ways, model_width)
    sectioned_in = jnp.take(sectioned_in, slot_order, axis=0)
    sectioned_down = jnp.take(sectioned_down, slot_order, axis=0)
    relaid_in, relaid_down = (
        lax.all_to_all(
            lax.all_to_all(sectioned_in, "dp", split_axis=2, concat_axis=3, tiled=True),
            "expert",
            split_axis=0,
            concat_axis=3,
            tiled=True,
        ),
        lax.all_to_all(
            lax.all_to_all(sectioned_down, "dp", split_axis=2, concat_axis=3, tiled=True),
            "expert",
            split_axis=0,
            concat_axis=3,
            tiled=True,
        ),
    )
    full_in, full_down = (
        lax.all_gather(relaid_in, "dp", axis=3, tiled=True),
        lax.all_gather(relaid_down, "dp", axis=3, tiled=True),
    )
    pair_in = full_in.reshape(2, -1, model_width)
    pair_down = full_down.reshape(-1, model_width)
    group_rows = lax.all_gather(own_rows, "shard", axis=0, tiled=True)
    summed = lax.psum_scatter(
        jnp.dot(
            swiglu_rows(group_rows, pair_in), pair_down, preferred_element_type=jnp.float32
        ).astype(jnp.bfloat16),
        "shard",
        scatter_dimension=0,
        tiled=True,
    )
    returned = lax.all_to_all(
        summed.reshape(experts, capacity, model_width),
        "expert",
        split_axis=0,
        concat_axis=0,
        tiled=True,
    )
    combine_weights = jnp.sum(cell_hits * gate_values[:, :, None], axis=1)
    mixed_out = jnp.dot(
        combine_weights,
        returned.reshape(cell_count, model_width).astype(jnp.float32),
        precision=lax.Precision.HIGHEST,
    )
    return mixed_out.astype(jnp.bfloat16)


def solution(mesh):
    in_specs = (
        P(("dp", "expert", "shard"), None),
        P(None, None, ("dp", "expert", "shard"), None),
        P(None, ("dp", "expert", "shard"), None),
        P(("dp", "expert", "shard"), None),
        P(("dp", "expert", "shard"), None),
        P(("dp", "expert", "shard"), None),
        P(),
        P(),
    )
    out_specs = P(("dp", "expert", "shard"), None)
    return jax.shard_map(local, mesh=mesh, in_specs=in_specs, out_specs=out_specs, check_vma=False)
```

profile of v0, /device:TPU:8, one launch (start us, length us, event | category | flops | bytes accessed | tf_op | source)
XLA Modules:
  0.0 681.6 jit_solution(10519561180992360223)
XLA Ops:
  8.3 1.2 convolution_convert_fusion.1
  9.5 0.9 reshape.64
  10.4 8.5 %all-to-all-start = ((bf16[8,4,6144]{2,1,0:T(4,128)(2,1)}), bf16[8,4,6144]{2,1,0:T(4,128)(2,1)S(1)}, u32[]{:S(2)}, u32[]{:S(2)}) async-start(bf16[8,4,6144]{2,1,0:T(4,128)(2,1)} %reshape.64), calls=%async_computation | async-start | bytes 786432 | tf_op jit(solution)/shard_map/all_to_all | solution.py:37
  19.7 6.4 gather_fusion
  26.1 3.5 broadcast_select_fusion
  29.6 3.1 copy.24
  33.5 6.3 all-to-all-start.1
  40.8 89.5 %all-to-all-done.1 = bf16[8,2,2,16,6144]{4,3,1,0,2:T(8,128)(2,1)} async-done(((bf16[8,2,2,16,6144]{4,3,1,0,2:T(8,128)(2,1)}), bf16[8,2,2,16,6144]{4,3,1,0,2:T(8,128)(2,1)}, u32[]{:S(2)}, u32[]{:S(2)}) %all-to-all-start.1) | async-done | bytes 6291488 | tf_op jit(solution)/shard_map/all_to_all | solution.py:51
  130.3 3.5 copy.25
  133.8 145.8 %all_to_all.64 = bf16[8,2,1,32,6144]{4,3,1,2,0:T(8,128)(2,1)S(1)} all-to-all(bf16[8,2,1,32,6144]{4,3,1,2,0:T(8,128)(2,1)S(1)} %bitcast.37), channel_id=1, replica_groups=mesh['dp'=2,'expert'=8,'shard'=16] {'expert'}, dimensions={0} | all-to-all | bytes 12582912 | tf_op jit(solution)/shard_map/all_to_all | solution.py:50
  279.7 3.1 copy.27
  282.8 2.4 gather_fusion.1
  285.3 2.3 bitcast_select_fusion
  287.9 63.1 %all_to_all.65 = bf16[8,1,2,16,6144]{4,3,0,1,2:T(8,128)(2,1)S(1)} all-to-all(bf16[8,1,2,16,6144]{4,3,0,1,2:T(8,128)(2,1)S(1)} %copy.28), channel_id=1, replica_groups=mesh['dp'=2,'expert'=8,'shard'=16] {'dp'}, dimensions={2} | all-to-all | bytes 6291456 | tf_op jit(solution)/shard_map/all_to_all | solution.py:58
  351.2 66.1 %all_to_all.66 = bf16[8,1,1,32,6144]{4,3,2,1,0:T(8,128)(2,1)} all-to-all(bf16[8,1,1,32,6144]{4,3,2,1,0:T(8,128)(2,1)S(1)} %bitcast.40), channel_id=1, replica_groups=mesh['dp'=2,'expert'=8,'shard'=16] {'expert'}, dimensions={0} | all-to-all | bytes 6291456 | tf_op jit(solution)/shard_map/all_to_all | solution.py:57
  417.5 41.2 %all-gather.6.cloned.1.call-done = bf16[1,2,1,512,6144]{4,3,1,2,0:T(8,128)(2,1)} async-done(((bf16[1,2,1,256,6144]{4,3,1,2,0:T(8,128)(2,1)}), bf16[1,2,1,512,6144]{4,3,1,2,0:T(8,128)(2,1)}) %all-gather.6.cloned.1.call-update) | async-done | bytes 12582928 | tf_op jit(solution)/shard_map/all_gather | solution.py:66
  458.6 12.5 %fusion = f32[512,2,512]{2,0,1:T(8,128)} fusion(bf16[1,2,1,512,6144]{4,3,1,2,0:T(8,128)(2,1)} %all-gather.6.cloned.1.call-done, bf16[512,6144]{1,0:T(8,128)(2,1)} %all-gather.4.cloned.1.call-done), kind=kOutput, calls=%fused_computation.2 | convolution fusion | flops 6442450944 | bytes 20971520 | tf_op jit(solution)/shard_map/rd,gud->rgu/dot_general | solution.py:14
  471.2 72.6 %all-gather.8.cloned.1.call-done = bf16[1,1,1,512,6144]{4,3,2,1,0:T(8,128)(2,1)} async-done(((bf16[1,1,1,256,6144]{4,3,2,1,0:T(8,128)(2,1)}), bf16[1,1,1,512,6144]{4,3,2,1,0:T(8,128)(2,1)}) %all-gather.8.cloned.1.call-update) | async-done | bytes 6291472 | tf_op jit(solution)/shard_map/all_gather | solution.py:67
  543.8 9.7 %convolution_convert_fusion = bf16[512,6144]{1,0:T(8,128)(2,1)} fusion(bf16[1,1,1,512,6144]{4,3,2,1,0:T(8,128)(2,1)} %all-gather.8.cloned.1.call-done, f32[512,2,512]{2,0,1:T(8,128)} %fusion), kind=kOutput, calls=%fused_computation.4 | convolution fusion | flops 3225944064 | bytes 14680064 | tf_op jit(solution)/shard_map/dot_general | solution.py:73
  553.6 98.3 %reduce-scatter.2.cloned.1.call-done = bf16[32,6144]{1,0:T(8,128)(2,1)} async-done(((bf16[512,6144]{1,0:T(8,128)(2,1)}), bf16[32,6144]{1,0:T(8,128)(2,1)}) %reduce-scatter.2.cloned.1.call-update) | async-done | bytes 393232 | tf_op jit(solution)/shard_map/reduce_scatter | solution.py:72
  651.9 1.1 reshape.70
  653.0 20.0 %all_to_all.67 = bf16[8,4,6144]{2,1,0:T(4,128)(2,1)} all-to-all(bf16[8,4,6144]{2,1,0:T(4,128)(2,1)S(1)} %reshape.70), channel_id=1, replica_groups=mesh['dp'=2,'expert'=8,'shard'=16] {'expert'}, dimensions={0} | all-to-all | bytes 786432 | tf_op jit(solution)/shard_map/all_to_all | solution.py:80
  673.1 1.1 reshape.71
  674.1 0.9 convolution_convert_fusion.2
  (23 shorter events, 5.2 us)
Async XLA Ops:
  6.5 276.3 %copy-start = (bf16[8,32,6144]{2,1,0:T(8,128)(2,1)S(1)}, bf16[8,32,6144]{2,1,0:T(8,128)(2,1)}, u32[]{:S(2)}) copy-start(bf16[8,32,6144]{2,1,0:T(8,128)(2,1)} %param.10) | copy-start | bytes 9437188
  10.4 23.2 %all-to-all-start = ((bf16[8,4,6144]{2,1,0:T(4,128)(2,1)}), bf16[8,4,6144]{2,1,0:T(4,128)(2,1)S(1)}, u32[]{:S(2)}, u32[]{:S(2)}) async-start(bf16[8,4,6144]{2,1,0:T(4,128)(2,1)} %reshape.64), calls=%async_computation | async-start | bytes 786432 | tf_op jit(solution)/shard_map/all_to_all | solution.py:37
  33.5 96.8 %all-to-all-start.1 = ((bf16[8,2,2,16,6144]{4,3,1,0,2:T(8,128)(2,1)}), bf16[8,2,2,16,6144]{4,3,1,0,2:T(8,128)(2,1)}, u32[]{:S(2)}, u32[]{:S(2)}) async-start(bf16[8,2,2,16,6144]{4,3,1,0,2:T(8,128)(2,1)} %copy.24), calls=%async_computation.1 | async-start | bytes 12582912 | tf_op jit(solution)/shard_map/all_to_all | solution.py:51
  39.8 377.6 %all-gather.4.cloned.1.call-start = ((), (), s32[]{:S(2)}) async-start(), calls=%async_computation.7 | async-start | bytes 6684672 | tf_op jit(solution)/shard_map/all_gather | solution.py:71
  40.8 417.9 %all-gather.6.cloned.1.call-start = ((), (), s32[]{:S(2)}) async-start(), calls=%async_computation.8 | async-start | bytes 18874368 | tf_op jit(solution)/shard_map/all_gather | solution.py:66
  282.8 261.0 %all-gather.8.cloned.1.call-start = ((), (), s32[]{:S(2)}) async-start(), calls=%async_computation.9 | async-start | bytes 9437184 | tf_op jit(solution)/shard_map/all_gather | solution.py:67
  417.4 234.5 %reduce-scatter.2.cloned.1.call-start = ((), (), s32[]{:S(2)}) async-start(), calls=%async_computation.10 | async-start | bytes 6684672 | tf_op jit(solution)/shard_map/reduce_scatter | solution.py:72
  543.8 131.2 %copy-start.1 = (bf16[8,32,6144]{2,1,0:T(8,128)(2,1)S(1)}, bf16[8,32,6144]{2,1,0:T(8,128)(2,1)}, u32[]{:S(2)}) copy-start(bf16[8,32,6144]{2,1,0:T(8,128)(2,1)} %param.10) | copy-start | bytes 9437188
Sparse Core Ops, SparseCore 0:
  43.4 90.1 all-gather.3
  282.9 175.6 all-gather.5
  460.4 83.3 all-gather.7
  553.7 98.1 reduce-scatter.1
where the time goes:
time: 682 us
  waiting for transfers between devices  303 us (44%)
  blocking collectives  295 us (43%)
  matrix products  24.3 us (4%)
  local copies, waits for them, and re-layouts  23.1 us (3%)
  starting transfers between devices  15 us (2%)
  between operations  13.2 us (2%)
  other arithmetic  8.31 us (1%)
    all_to_all x1, blocking collectives, local(): lax.all_to_all(lax.all_to_all(sectioned_in, 'dp', split_axis=2, concat_ax...  146 us
    reduce_scatter x1, waiting for transfers between devices, local(): lax.psum_scatter(jnp.dot(swiglu_rows(group_rows, pair_in), pair_down, pre...  98.3 us
    all_to_all x1, waiting for transfers between devices, local(): lax.all_to_all(sectioned_in, 'dp', split_axis=2, concat_axis=3, tiled=True)  89.5 us
    all_gather x1, waiting for transfers between devices, local(): lax.all_gather(relaid_down, 'dp', axis=3, tiled=True)  72.6 us
    all_to_all x1, blocking collectives, local(): lax.all_to_all(lax.all_to_all(sectioned_down, 'dp', split_axis=2, concat_...  66.1 us
    all_to_all x1, blocking collectives, local(): lax.all_to_all(sectioned_down, 'dp', split_axis=2, concat_axis=3, tiled=T...  63.1 us
    all_gather x1, waiting for transfers between devices, local(): lax.all_gather(relaid_in, 'dp', axis=3, tiled=True)  41.2 us
    all_to_all x1, blocking collectives, local(): lax.all_to_all(summed.reshape(experts, capacity, model_width), 'expert',...  20 us
  transfers between devices with their start and end apart: 6, of which 5 were waited for; matrix products, arithmetic and copies ran while one was open for 6% of the time, Pallas kernels for 0%

commit v1 on v0

--- a/solution.py
+++ b/solution.py
@@ -2,6 +2,28 @@
 import jax.numpy as jnp
 from jax import lax
 from jax.sharding import PartitionSpec as P
+
+
+def in_blocks(x, dim, size):
+    before, after = (x.shape[:dim], x.shape[dim + 1 :])
+    return jnp.moveaxis(x.reshape(*before, size, -1, *after), dim, 0)
+
+
+def laid_out(blocks, dim):
+    blocks = jnp.moveaxis(blocks, 0, dim)
+    dims = blocks.shape
+    return blocks.reshape(*dims[:dim], dims[dim] * dims[dim + 1], *dims[dim + 2 :])
+
+
+def exchange_in_pairs(shard, axis, split_dim, concat_dim):
+    devices, here = (lax.axis_size(axis), lax.axis_index(axis))
+    tiles = in_blocks(shard, split_dim, devices)
+    outs = [tiles[here]]
+    for lap in range(1, devices):
+        sent = tiles[here ^ lap]
+        outs.append(lax.ppermute(sent, axis, [(i, i ^ lap) for i in range(devices)]))
+    tiles = jnp.stack(outs)[here ^ jnp.arange(devices)]
+    return laid_out(tiles, concat_dim)
 
 
 def placement_order(old_place, new_place):
@@ -54,12 +76,11 @@
             concat_axis=3,
             tiled=True,
         ),
-        lax.all_to_all(
+        exchange_in_pairs(
             lax.all_to_all(sectioned_down, "dp", split_axis=2, concat_axis=3, tiled=True),
             "expert",
-            split_axis=0,
-            concat_axis=3,
-            tiled=True,
+            0,
+            3,
         ),
     )
     full_in, full_down = (

time: 682 us -> 690 us (1.012)
  blocking collectives: 295 us -> 20 us
  waiting for transfers between devices: 303 us -> 558 us
  starting transfers between devices: 15 us -> 33.6 us
  local copies, waits for them, and re-layouts: 23.1 us -> 35.5 us
    all_to_all x3 -> x0, blocking collectives: 275 us -> none  [the longest x1 146 us: local(): lax.all_to_all(lax.all_to_all(sectioned_in, 'dp', split_axis=2, concat_ax...]
    all_to_all x0 -> x2, waiting for transfers between devices: none -> 202 us  [the longest x1 137 us: local(): lax.all_to_all(lax.all_to_all(sectioned_in, 'dp', split_axis=2, concat_ax...]
    ppermute x0 -> x7, waiting for transfers between devices: none -> 63.7 us  [exchange_in_pairs(): lax.ppermute(sent, axis, [(i, i ^ lap) for i in range(devices)])]
    all_to_all x0 -> x2, starting transfers between devices: none -> 10.4 us  [the longest x1 6.4 us: local(): lax.all_to_all(lax.all_to_all(sectioned_in, 'dp', split_axis=2, concat_ax...]
    all_gather x1, waiting for transfers between devices: 41.2 us -> 31.8 us  [local(): lax.all_gather(relaid_in, 'dp', axis=3, tiled=True)]
    ppermute x0 -> x7, starting transfers between devices: none -> 8.14 us  [exchange_in_pairs(): lax.ppermute(sent, axis, [(i, i ^ lap) for i in range(devices)])]
  transfers between devices with their start and end apart: 6 -> 15, of which waited for: 5 -> 12; matrix products, arithmetic and copies ran while one was open for 6% -> 7% of each run, Pallas kernels for 0% -> 0%
where the time goes in v1:
time: 690 us; the launch traced here: 689 us
  waiting for transfers between devices  558 us (81%)
  local copies, waits for them, and re-layouts  35.5 us (5%)
  starting transfers between devices  33.6 us (5%)
  matrix products  21.8 us (3%)
  blocking collectives  20 us (3%)
  between operations  13.4 us (2%)
    all_to_all x1, waiting for transfers between devices, local(): lax.all_to_all(lax.all_to_all(sectioned_in, 'dp', split_axis=2, concat_ax...  137 us
    reduce_scatter x1, waiting for transfers between devices, local(): lax.psum_scatter(jnp.dot(swiglu_rows(group_rows, pair_in), pair_down, pre...  98.4 us
    all_to_all x1, waiting for transfers between devices, local(): lax.all_to_all(sectioned_in, 'dp', split_axis=2, concat_axis=3, tiled=True)  89.6 us
    all_gather x1, waiting for transfers between devices, local(): lax.all_gather(relaid_down, 'dp', axis=3, tiled=True)  71.8 us
    all_to_all x1, waiting for transfers between devices, local(): lax.all_to_all(sectioned_down, 'dp', split_axis=2, concat_axis=3, tiled=T...  64.3 us
    ppermute x7, waiting for transfers between devices, exchange_in_pairs(): lax.ppermute(sent, axis, [(i, i ^ lap) for i in range(devices)])  63.7 us
    all_gather x1, waiting for transfers between devices, local(): lax.all_gather(relaid_in, 'dp', axis=3, tiled=True)  31.8 us
    all_to_all x1, blocking collectives, local(): lax.all_to_all(summed.reshape(experts, capacity, model_width), 'expert',...  20 us
  transfers between devices with their start and end apart: 15, of which 12 were waited for; matrix products, arithmetic and copies ran while one was open for 7% of the time, Pallas kernels for 0%

profile of v1, /device:TPU:8, one launch (start us, length us, event | category | flops | bytes accessed | tf_op | source)
XLA Modules:
  0.0 688.8 jit_solution(6858398019625500374)
XLA Ops:
  10.4 8.5 %all-to-all-start = ((bf16[8,4,6144]{2,1,0:T(4,128)(2,1)}), bf16[8,4,6144]{2,1,0:T(4,128)(2,1)S(1)}, u32[]{:S(2)}, u32[]{:S(2)}) async-start(bf16[8,4,6144]{2,1,0:T(4,128)(2,1)} %reshape.81), calls=%async_computation | async-start | bytes 786432 | tf_op jit(solution)/shard_map/all_to_all | solution.py:59
  19.7 6.4 gather_fusion
  26.1 3.5 broadcast_select_fusion
  33.5 6.3 all-to-all-start.1
  40.8 89.6 %all-to-all-done.1 = bf16[8,2,2,16,6144]{4,3,1,0,2:T(8,128)(2,1)} async-done(((bf16[8,2,2,16,6144]{4,3,1,0,2:T(8,128)(2,1)}), bf16[8,2,2,16,6144]{4,3,1,0,2:T(8,128)(2,1)}, u32[]{:S(2)}, u32[]{:S(2)}) %all-to-all-start.1) | async-done | bytes 6291488 | tf_op jit(solution)/shard_map/all_to_all | solution.py:73
  130.3 6.4 copy.24
  136.8 6.4 all-to-all-start.2
  145.7 137.5 %all-to-all-done.2 = bf16[8,2,1,32,6144]{4,3,1,2,0:T(8,128)(2,1)} async-done(((bf16[8,2,1,32,6144]{4,3,1,2,0:T(8,128)(2,1)}), bf16[8,2,1,32,6144]{4,3,1,2,0:T(8,128)(2,1)}, u32[]{:S(2)}, u32[]{:S(2)}) %all-to-all-start.2) | async-done | bytes 6291488 | tf_op jit(solution)/shard_map/all_to_all | solution.py:72
  283.2 6.1 copy.26
  293.6 4.0 all-to-all-start.3
  297.7 64.3 %all-to-all-done.3 = bf16[8,1,2,16,6144]{4,3,0,1,2:T(8,128)(2,1)S(1)} async-done(((bf16[8,1,2,16,6144]{4,3,0,1,2:T(8,128)(2,1)}), bf16[8,1,2,16,6144]{4,3,0,1,2:T(8,128)(2,1)S(1)}, u32[]{:S(2)}, u32[]{:S(2)}) %all-to-all-start.3) | async-done | bytes 3145760 | tf_op jit(solution)/shard_map/all_to_all | solution.py:80
  362.8 4.3 collective-permute-start.2
  367.1 3.6 collective-permute-start.4
  370.7 15.6 %collective-permute-done = bf16[1,1,1,32,6144]{4,3,2,1,0:T(8,128)(2,1)S(1)} collective-permute-done((bf16[1,1,1,32,6144]{4,3,2,1,0:T(8,128)(2,1)S(1)}, bf16[1,1,1,32,6144]{4,3,2,1,0:T(8,128)(2,1)S(1)}, u32[]{:S(2)}, u32[]{:S(2)}) %collective-permute-start) | collective-permute-done | bytes 393248 | tf_op jit(solution)/shard_map/ppermute | solution.py:24
  386.3 24.6 %collective-permute-done.1 = bf16[1,1,1,32,6144]{4,3,2,1,0:T(8,128)(2,1)S(1)} collective-permute-done((bf16[1,1,1,32,6144]{4,3,2,1,0:T(8,128)(2,1)S(1)}, bf16[1,1,1,32,6144]{4,3,2,1,0:T(8,128)(2,1)S(1)}, u32[]{:S(2)}, u32[]{:S(2)}) %collective-permute-start.1) | collective-permute-done | bytes 393248 | tf_op jit(solution)/shard_map/ppermute | solution.py:24
  411.0 9.3 %collective-permute-done.2 = bf16[1,1,1,32,6144]{4,3,2,1,0:T(8,128)(2,1)S(1)} collective-permute-done((bf16[1,1,1,32,6144]{4,3,2,1,0:T(8,128)(2,1)S(1)}, bf16[1,1,1,32,6144]{4,3,2,1,0:T(8,128)(2,1)S(1)}, u32[]{:S(2)}, u32[]{:S(2)}) %collective-permute-start.2) | collective-permute-done | bytes 393248 | tf_op jit(solution)/shard_map/ppermute | solution.py:24
  420.3 6.6 collective-permute-done.3
  427.0 7.6 %collective-permute-done.6 = bf16[1,1,1,32,6144]{4,3,2,1,0:T(8,128)(2,1)S(1)} collective-permute-done((bf16[1,1,1,32,6144]{4,3,2,1,0:T(8,128)(2,1)S(1)}, bf16[1,1,1,32,6144]{4,3,2,1,0:T(8,128)(2,1)S(1)}, u32[]{:S(2)}, u32[]{:S(2)}) %collective-permute-start.6) | collective-permute-done | bytes 393248 | tf_op jit(solution)/shard_map/ppermute | solution.py:24
  437.3 31.8 %all-gather.6.cloned.1.call-done = bf16[1,2,1,512,6144]{4,3,1,2,0:T(8,128)(2,1)} async-done(((bf16[1,2,1,256,6144]{4,3,1,2,0:T(8,128)(2,1)}), bf16[1,2,1,512,6144]{4,3,1,2,0:T(8,128)(2,1)}) %all-gather.6.cloned.1.call-update) | async-done | bytes 12582928 | tf_op jit(solution)/shard_map/all_gather | solution.py:87
  469.1 11.6 %fusion = f32[512,2,512]{2,0,1:T(8,128)S(1)} fusion(bf16[1,2,1,512,6144]{4,3,1,2,0:T(8,128)(2,1)} %all-gather.6.cloned.1.call-done, bf16[512,6144]{1,0:T(8,128)(2,1)} %all-gather.4.cloned.1.call-done), kind=kOutput, calls=%fused_computation.3 | convolution fusion | flops 6442450944 | bytes 20971520 | tf_op jit(solution)/shard_map/rd,gud->rgu/dot_general | solution.py:36
  480.7 71.8 %all-gather.8.cloned.1.call-done = bf16[1,1,1,512,6144]{4,3,2,1,0:T(8,128)(2,1)} async-done(((bf16[1,1,1,256,6144]{4,3,2,1,0:T(8,128)(2,1)}), bf16[1,1,1,512,6144]{4,3,2,1,0:T(8,128)(2,1)}) %all-gather.8.cloned.1.call-update) | async-done | bytes 6291472 | tf_op jit(solution)/shard_map/all_gather | solution.py:88
  552.5 8.1 %convolution_convert_fusion = bf16[512,6144]{1,0:T(8,128)(2,1)} fusion(bf16[1,1,1,512,6144]{4,3,2,1,0:T(8,128)(2,1)} %all-gather.8.cloned.1.call-done, f32[512,2,512]{2,0,1:T(8,128)S(1)} %fusion), kind=kOutput, calls=%fused_computation.5 | convolution fusion | flops 3225944064 | bytes 14680064 | tf_op jit(solution)/shard_map/dot_general | solution.py:94
  560.7 98.4 %reduce-scatter.2.cloned.1.call-done = bf16[32,6144]{1,0:T(8,128)(2,1)} async-done(((bf16[512,6144]{1,0:T(8,128)(2,1)}), bf16[32,6144]{1,0:T(8,128)(2,1)}) %reduce-scatter.2.cloned.1.call-update) | async-done | bytes 393232 | tf_op jit(solution)/shard_map/reduce_scatter | solution.py:93
  660.2 20.0 %all_to_all.49 = bf16[8,4,6144]{2,1,0:T(4,128)(2,1)} all-to-all(bf16[8,4,6144]{2,1,0:T(4,128)(2,1)S(1)} %reshape.88), channel_id=1, replica_groups=mesh['dp'=2,'expert'=8,'shard'=16] {'expert'}, dimensions={0} | all-to-all | bytes 786432 | tf_op jit(solution)/shard_map/all_to_all | solution.py:101
  (51 shorter events, 23.2 us)
Async XLA Ops:
  6.5 136.7 %copy-start = (bf16[8,32,6144]{2,1,0:T(8,128)(2,1)S(1)}, bf16[8,32,6144]{2,1,0:T(8,128)(2,1)}, u32[]{:S(2)}) copy-start(bf16[8,32,6144]{2,1,0:T(8,128)(2,1)} %param.10) | copy-start | bytes 9437188
  10.4 23.1 %all-to-all-start = ((bf16[8,4,6144]{2,1,0:T(4,128)(2,1)}), bf16[8,4,6144]{2,1,0:T(4,128)(2,1)S(1)}, u32[]{:S(2)}, u32[]{:S(2)}) async-start(bf16[8,4,6144]{2,1,0:T(4,128)(2,1)} %reshape.81), calls=%async_computation | async-start | bytes 786432 | tf_op jit(solution)/shard_map/all_to_all | solution.py:59
  33.5 96.8 %all-to-all-start.1 = ((bf16[8,2,2,16,6144]{4,3,1,0,2:T(8,128)(2,1)}), bf16[8,2,2,16,6144]{4,3,1,0,2:T(8,128)(2,1)}, u32[]{:S(2)}, u32[]{:S(2)}) async-start(bf16[8,2,2,16,6144]{4,3,1,0,2:T(8,128)(2,1)} %copy.23), calls=%async_computation.1 | async-start | bytes 12582912 | tf_op jit(solution)/shard_map/all_to_all | solution.py:73
  39.8 397.5 %all-gather.4.cloned.1.call-start = ((), (), s32[]{:S(2)}) async-start(), calls=%async_computation.6 | async-start | bytes 6684672 | tf_op jit(solution)/shard_map/all_gather | solution.py:92
  136.8 146.4 %all-to-all-start.2 = ((bf16[8,2,1,32,6144]{4,3,1,2,0:T(8,128)(2,1)}), bf16[8,2,1,32,6144]{4,3,1,2,0:T(8,128)(2,1)}, u32[]{:S(2)}, u32[]{:S(2)}) async-start(bf16[8,2,1,32,6144]{4,3,1,2,0:T(8,128)(2,1)} %bitcast.66), calls=%async_computation.2 | async-start | bytes 12582912 | tf_op jit(solution)/shard_map/all_to_all | solution.py:72
  143.2 326.0 %all-gather.6.cloned.1.call-start = ((), (), s32[]{:S(2)}) async-start(), calls=%async_computation.7 | async-start | bytes 18874368 | tf_op jit(solution)/shard_map/all_gather | solution.py:87
  289.3 1.9 copy-start.2
  293.6 68.4 %all-to-all-start.3 = ((bf16[8,1,2,16,6144]{4,3,0,1,2:T(8,128)(2,1)}), bf16[8,1,2,16,6144]{4,3,0,1,2:T(8,128)(2,1)S(1)}, u32[]{:S(2)}, u32[]{:S(2)}) async-start(bf16[8,1,2,16,6144]{4,3,0,1,2:T(8,128)(2,1)} %copy.27), calls=%async_computation.3 | async-start | bytes 6291456 | tf_op jit(solution)/shard_map/all_to_all | solution.py:80
  297.6 254.9 %all-gather.8.cloned.1.call-start = ((), (), s32[]{:S(2)}) async-start(), calls=%async_computation.8 | async-start | bytes 9437184 | tf_op jit(solution)/shard_map/all_gather | solution.py:88
  362.5 23.7 %collective-permute-start = (bf16[1,1,1,32,6144]{4,3,2,1,0:T(8,128)(2,1)S(1)}, bf16[1,1,1,32,6144]{4,3,2,1,0:T(8,128)(2,1)S(1)}, u32[]{:S(2)}, u32[]{:S(2)}) collective-permute-start(bf16[1,1,1,32,6144]{4,3,2,1,0:T(8,128)(2,1)S(1)} %get-tuple-element.13), channel_id=1, source_target_pairs={{0,16},{16,0},{32,48},{48,32},{64,80},{80,64},{96,112},{112,96},{1... | collective-permute-start | bytes 1179656 | tf_op jit(solution)/shard_map/ppermute | solution.py:24
  362.7 48.2 %collective-permute-start.1 = (bf16[1,1,1,32,6144]{4,3,2,1,0:T(8,128)(2,1)S(1)}, bf16[1,1,1,32,6144]{4,3,2,1,0:T(8,128)(2,1)S(1)}, u32[]{:S(2)}, u32[]{:S(2)}) collective-permute-start(bf16[1,1,1,32,6144]{4,3,2,1,0:T(8,128)(2,1)S(1)} %get-tuple-element.12), channel_id=1, source_target_pairs={{0,32},{16,48},{32,0},{48,16},{64,96},{80,112},{96,64},{112,80},{1... | collective-permute-start | bytes 1179656 | tf_op jit(solution)/shard_map/ppermute | solution.py:24
  362.8 57.5 %collective-permute-start.2 = (bf16[1,1,1,32,6144]{4,3,2,1,0:T(8,128)(2,1)S(1)}, bf16[1,1,1,32,6144]{4,3,2,1,0:T(8,128)(2,1)S(1)}, u32[]{:S(2)}, u32[]{:S(2)}) collective-permute-start(bf16[1,1,1,32,6144]{4,3,2,1,0:T(8,128)(2,1)S(1)} %get-tuple-element.11), channel_id=1, source_target_pairs={{0,48},{16,32},{32,16},{48,0},{64,112},{80,96},{96,80},{112,64},{1... | collective-permute-start | bytes 1179656 | tf_op jit(solution)/shard_map/ppermute | solution.py:24
  367.1 59.8 %collective-permute-start.3 = (bf16[1,1,1,32,6144]{4,3,2,1,0:T(8,128)(2,1)S(1)}, bf16[1,1,1,32,6144]{4,3,2,1,0:T(8,128)(2,1)S(1)}, u32[]{:S(2)}, u32[]{:S(2)}) collective-permute-start(bf16[1,1,1,32,6144]{4,3,2,1,0:T(8,128)(2,1)S(1)} %get-tuple-element.10), channel_id=1, source_target_pairs={{0,64},{16,80},{32,96},{48,112},{64,0},{80,16},{96,32},{112,48},{1... | collective-permute-start | bytes 1179656 | tf_op jit(solution)/shard_map/ppermute | solution.py:24
  367.1 59.8 %collective-permute-start.4 = (bf16[1,1,1,32,6144]{4,3,2,1,0:T(8,128)(2,1)S(1)}, bf16[1,1,1,32,6144]{4,3,2,1,0:T(8,128)(2,1)S(1)}, u32[]{:S(2)}, u32[]{:S(2)}) collective-permute-start(bf16[1,1,1,32,6144]{4,3,2,1,0:T(8,128)(2,1)S(1)} %get-tuple-element.9), channel_id=1, source_target_pairs={{0,80},{16,64},{32,112},{48,96},{64,16},{80,0},{96,48},{112,32},{1... | collective-permute-start | bytes 1179656 | tf_op jit(solution)/shard_map/ppermute | solution.py:24
  386.3 40.7 %collective-permute-start.5 = (bf16[1,1,1,32,6144]{4,3,2,1,0:T(8,128)(2,1)S(1)}, bf16[1,1,1,32,6144]{4,3,2,1,0:T(8,128)(2,1)S(1)}, u32[]{:S(2)}, u32[]{:S(2)}) collective-permute-start(bf16[1,1,1,32,6144]{4,3,2,1,0:T(8,128)(2,1)S(1)} %get-tuple-element.8), channel_id=1, source_target_pairs={{0,96},{16,112},{32,64},{48,80},{64,32},{80,48},{96,0},{112,16},{1... | collective-permute-start | bytes 1179656 | tf_op jit(solution)/shard_map/ppermute | solution.py:24
  410.9 23.7 %collective-permute-start.6 = (bf16[1,1,1,32,6144]{4,3,2,1,0:T(8,128)(2,1)S(1)}, bf16[1,1,1,32,6144]{4,3,2,1,0:T(8,128)(2,1)S(1)}, u32[]{:S(2)}, u32[]{:S(2)}) collective-permute-start(bf16[1,1,1,32,6144]{4,3,2,1,0:T(8,128)(2,1)S(1)} %get-tuple-element.7), channel_id=1, source_target_pairs={{0,112},{16,96},{32,80},{48,64},{64,48},{80,32},{96,16},{112,0},{1... | collective-permute-start | bytes 1179656 | tf_op jit(solution)/shard_map/ppermute | solution.py:24
  437.1 222.0 %reduce-scatter.2.cloned.1.call-start = ((), (), s32[]{:S(2)}) async-start(), calls=%async_computation.9 | async-start | bytes 6684672 | tf_op jit(solution)/shard_map/reduce_scatter | solution.py:93
  560.7 121.6 %copy-start.1 = (bf16[8,32,6144]{2,1,0:T(8,128)(2,1)S(1)}, bf16[8,32,6144]{2,1,0:T(8,128)(2,1)}, u32[]{:S(2)}) copy-start(bf16[8,32,6144]{2,1,0:T(8,128)(2,1)} %param.10) | copy-start | bytes 9437188
Sparse Core Ops, SparseCore 0:
  43.4 90.1 all-gather.3
  289.4 179.6 all-gather.5
  470.9 81.5 all-gather.7
  560.8 98.1 reduce-scatter.1
